TPU v7x, 32 devices: a whole 2x2x4 slice. The times are simulated.
32 devices in a mesh: groups: 2 (over y), seq: 4 (over z), tp: 2 (over x), kv: 2 (over core).
Axes of the slice: x: 2, y: 2, z: 4, core: 2. Of those that a mesh axis runs over, the one named last changes fastest.
Arguments:
- events: bfloat16 [8, 512, 2048], P('groups', 'seq', ('tp', 'kv')), parts along dimension 0, may hold values from -6 to 6
- history_cache: bfloat16 [2, 8, 512, 1024], P(None, ('groups', 'seq'), None, ('tp', 'kv')), parts along dimension 1, may hold values from -6 to 6
- block_counts: int32 [8], P(('groups', 'seq')), parts along dimension 0, may hold values from 1 to 4
- semantic_ids: int32 [4, 128], P(None, ('groups', 'seq')), parts along dimension 1, may hold values from 0 to 4095
- beam_parents: int32 [3, 128], P(None, ('groups', 'seq')), parts along dimension 1, may hold values from 0 to 15
- query_weight: bfloat16 [2048, 2048], P('seq', ('tp', 'kv')), may hold values from -0.125 to 0.125
- keyval_weight: bfloat16 [2, 2048, 1024], P(None, 'seq', ('tp', 'kv')), may hold values from -0.125 to 0.125
- out_weight: bfloat16 [2048, 2048], P('seq', ('tp', 'kv')), may hold values from -0.125 to 0.125
- cross_weight: bfloat16 [2, 2048, 1024], P(None, 'seq', ('tp', 'kv')), may hold values from -0.125 to 0.125
- decoder_query: bfloat16 [2048, 2048], P(None, ('tp', 'kv')), may hold values from -0.125 to 0.125
- decoder_out: bfloat16 [2048, 2048], P(None, ('tp', 'kv')), may hold values from -0.125 to 0.125
- code_table: bfloat16 [4096, 2048], P(('tp', 'kv')), may hold values from -6 to 6
- encoder_gain: float32 [2048], replicated, may hold values from 0.25 to 1.75
- cross_gain: float32 [2048], replicated, may hold values from 0.25 to 1.75
- decoder_gain: float32 [2048], replicated, may hold values from 0.25 to 1.75
Outputs:
- encoded: bfloat16 [8, 512, 2048], P(('groups', 'seq'), ('tp', 'kv')), parts along dimension 0
- beam_state: bfloat16 [128, 2048], P(('groups', 'seq'), ('tp', 'kv')), parts along dimension 0
There are 2 independent parts, one for each index of `groups`. A program takes and returns all parts, laid end to end along the dimension named above; an argument that names none is the same for every part. Nothing has to cross between parts.
Inputs may be any that keep to these rules, and one draw needn't show every extreme that they name: A user's first 128 * block_counts new events are real; the rest are padding. `semantic_ids`: the codebook entry decoded for each beam row. `beam_parents`: the beam of the previous step that each beam row continues, counted among its user's 16 beams.
All inputs are finite; a program needn't handle non-finite values.
Results may differ from a plain program's by a relative error of at most 0.014.
Values may be sent and summed in bfloat16 or wider, within the bound.
A program may use at most 64 MiB of HBM per device.

v0:
```python
import functools

import jax
import jax.numpy as jnp
from jax import lax
from jax.experimental import pallas as pl
from jax.experimental.pallas import tpu as pltpu
from jax.sharding import PartitionSpec as P

DH = 128
BLK = 128
eps = 1e-06
F32 = jnp.float32
BF16 = jnp.bfloat16
MESH = pl.DeviceIdType.MESH


def unit(values):
    return lax.rsqrt(jnp.mean(values * values, axis=-1, keepdims=True) + eps)


def dot(a, b):
    return jnp.dot(a, b, preferred_element_type=F32)


def dot_t(a, b):
    return lax.dot_general(a, b, (((1,), (1,)), ((), ())), preferred_element_type=F32)


def body(
    sizes,
    events, history, counts, ids, parents, wq_in, wkv_in, wo_in, wc_in, dq_in, do_in, table_in,
    egain, cgain, dgain,
    enc_out, beam_out,
    wq, wkv, wo, wc, dq, do, table, hist, xb, normed, qs, kn, vn, att, gterm, rk, s1, rt, cx, ck, cv,
    look, terms, last_own, last_in, hidden_ref, mixed_ref, ba, old,
    local_sem, z_send, z_recv, y_send, y_recv, ev_send, ev_recv,
    ag_send, ag_recv, lk_send, lk_recv, rk_send, rk_recv, rt_send, rt_recv, tm_send, tm_recv,
):
    G, S, T, K = sizes
    TK = T * K
    g, s = lax.axis_index("groups"), lax.axis_index("seq")
    t, k = lax.axis_index("tp"), lax.axis_index("kv")
    p = t * K + k
    rows = wq_in.shape[0]
    part = rows // G
    width = wq.shape[0]
    length = normed.shape[0]
    block = length // S
    share = length // TK
    cols = wq.shape[1]
    kcols = kn.shape[1]
    beams = hidden_ref.shape[0]
    steps = ids.shape[0]
    pending = []

    def when(condition, action):
        if condition is True:
            action()
        else:
            pl.when(condition)(action)

    def send(make, condition=True):
        when(condition, lambda: make().start())
        pending.append((make, condition))

    def remote(src, dst, ss, rs, **where):
        return pltpu.make_async_remote_copy(
            src_ref=src, dst_ref=dst, send_sem=ss, recv_sem=rs, device_id=where, device_id_type=MESH
        )

    barrier = pltpu.get_barrier_semaphore()
    for j in range(1, S):
        pl.semaphore_signal(barrier, inc=1, device_id={"seq": lax.rem(s + j, S)}, device_id_type=MESH)
    for j in range(1, G):
        pl.semaphore_signal(barrier, inc=1, device_id={"groups": lax.rem(g + j, G)}, device_id_type=MESH)
    peers = []
    for j in range(1, TK):
        other = lax.rem(p + j, TK)
        peers.append((j - 1, other, lax.div(other, K), lax.rem(other, K)))
        pl.semaphore_signal(
            barrier, inc=1, device_id={"tp": peers[-1][2], "kv": peers[-1][3]}, device_id_type=MESH
        )

    mine = pl.ds(pl.multiple_of(s * rows, rows), rows)
    stay = pl.ds(pl.multiple_of(s * block, block), block)
    local = [
        pltpu.make_async_copy(a, b, local_sem.at[i])
        for i, (a, b) in enumerate(
            [
                (events.at[s], xb.at[p, stay]),
                (wq_in, wq.at[mine]),
                (wkv_in, wkv.at[:, mine]),
                (table_in, table),
                (history.at[:, 0], hist),
                (wo_in, wo.at[mine]),
                (wc_in, wc.at[:, mine]),
                (dq_in, dq),
                (do_in, do),
            ]
        )
    ]
    for copy in local:
        copy.start()
    pl.semaphore_wait(barrier, (S - 1) + (G - 1) + (TK - 1))

    for j in range(1, S):

        def make(j=j):
            to = lax.rem(s + j, S)
            return remote(
                events.at[to], xb.at[p, stay], ev_send.at[j - 1], ev_recv.at[j - 1], seq=to
            )

        send(make)

    arrays = [
        (wq, wq_in, None, 0, 2), (wq, wq_in, None, 1, 2),
        (wkv, wkv_in, 0, 0, 1), (wkv, wkv_in, 1, 0, 1),
        (wo, wo_in, None, 0, 2), (wo, wo_in, None, 1, 2),
        (wc, wc_in, slice(None), 0, 1),
    ]

    def cut(ref, array, start):
        lead, sub, of = arrays[array][2:]
        size = part // of
        where = pl.ds(pl.multiple_of(start + sub * size, size), size)
        return ref.at[where] if lead is None else ref.at[lead, where]

    def at(array, origin, which):
        return cut(arrays[array][0], array, origin * rows + which * part)

    def own(array):
        return cut(arrays[array][1], array, g * part)

    def there(side, r):
        return s - r >= 0 if side == 0 else s + r < S

    def hop(array, side, r):
        step = 1 if side == 0 else -1

        def make():
            origin = s - step * r
            src = own(array) if r == 0 else at(array, origin, g)
            return remote(
                src, at(array, origin, g), z_send.at[array, side, r], z_recv.at[array, side, r], seq=s + step
            )

        ok = s + step < S if side == 0 else s + step >= 0
        if r > 0:
            ok = jnp.logical_and(ok, there(side, r))
        send(make, ok)

    def across(array, side, r):
        step = 1 if side == 0 else -1
        for j in range(1, G):

            def make(j=j):
                piece = at(array, s - step * r, g)
                return remote(
                    piece, piece, y_send.at[array, side, r, j - 1], y_recv.at[array, side, r, j - 1],
                    groups=lax.rem(g + j, G),
                )

            send(make, there(side, r))

    def arrive(array, r):
        for side in (0, 1):
            step = 1 if side == 0 else -1

            def wait(side=side, step=step):
                piece = at(array, s - step * r, g)
                remote(
                    piece, piece, z_send.at[array, side, r - 1], z_recv.at[array, side, r - 1], seq=s
                ).wait_recv()

            when(there(side, r), wait)
            if r + 1 < S:
                hop(array, side, r)
            across(array, side, r)

    def settle(array):
        for r in range(1, S):
            for side in (0, 1):
                step = 1 if side == 0 else -1

                def wait(side=side, step=step, r=r):
                    for j in range(1, G):
                        piece = at(array, s - step * r, lax.rem(g - j + G, G))
                        remote(
                            piece, piece, y_send.at[array, side, r, j - 1], y_recv.at[array, side, r, j - 1],
                            groups=g,
                        ).wait_recv()

                when(there(side, r), wait)

    def begin(array):
        hop(array, 0, 0)
        hop(array, 1, 0)

    stages = [(0, 1), (2, 3), (4, 5), (6,)]
    order = [("begin", a, 0) for a in stages[0]]
    for n, stage in enumerate(stages):
        for r in range(1, S):
            order += [("arrive", a, r) for a in stage]
            if r == max(S - 2, 1) and n + 1 < len(stages):
                order += [("begin", a, 0) for a in stages[n + 1]]
    progress = [0]

    def upto(stage, r):
        goal = max(
            i for i, (what, a, level) in enumerate(order)
            if (what == "arrive" and a in stages[stage] and level <= r)
            or (what == "begin" and stage + 1 < len(stages) and a in stages[stage + 1] and r >= max(S - 2, 1))
            or (what == "begin" and a in stages[stage])
        )
        while progress[0] <= goal:
            what, a, level = order[progress[0]]
            if what == "begin":
                begin(a)
            else:
                arrive(a, level)
            progress[0] += 1

    near, far, end = max(S - 3, 1), max(S - 2, 1), S - 1
    upto(0, 0)

    def spread(buffer, base, lines):
        def give(source, slot, **where):
            def make():
                piece = buffer.at[source, lines]
                return remote(piece, piece, ag_send.at[base, slot], ag_recv.at[base, slot], **where)

            send(make)

        def take(source, slot):
            piece = buffer.at[source, lines]
            remote(piece, piece, ag_send.at[base, slot], ag_recv.at[base, slot], tp=t).wait_recv()

        for i in range(1, T):
            give(p, i, tp=lax.rem(t + i, T))
        for j in range(1, K):
            give(p, T * j, kv=lax.rem(k + j, K))

        def relay():
            for i in range(1, T):
                there = lax.rem(t - i + T, T) * K + k
                take(there, i)
                for j in range(1, K):
                    give(there, T * j + i, kv=lax.rem(k + j, K))

        def finish():
            for j in range(1, K):
                for i in range(T):
                    there = lax.rem(t - i + T, T) * K + lax.rem(k - j + K, K)
                    take(there, T * j + i)

        return relay, finish

    moves = []
    for j in range(S):
        came = pl.ds(pl.multiple_of(lax.rem(s - j + S, S) * block, block), block)
        if j == 0:
            local[0].wait()
        else:
            piece = xb.at[p, came]
            remote(piece, piece, ev_send.at[j - 1], ev_recv.at[j - 1], seq=s).wait_recv()
        moves.append(spread(xb, j, came) + (came,))

    local[3].wait()
    vocab = table.shape[0]
    column = jnp.zeros((steps * beams, 1), jnp.int32)
    line = lax.broadcasted_iota(jnp.int32, column.shape, 0)
    for r in range(steps * beams):
        column = jnp.where(line == r, ids[r // beams, r % beams], column)
    onehot = (
        column == p * vocab + lax.broadcasted_iota(jnp.int32, (steps * beams, vocab), 1)
    ).astype(BF16)
    for c in range(TK):
        span = slice(c * cols, (c + 1) * cols)
        look[p, :, span] = dot(onehot, table[:, span]).astype(BF16)

    upto(0, near)
    for relay, finish, came in moves:
        relay()
    for slot, other, pt, pk in peers:

        def make(slot=slot, pt=pt, pk=pk):
            return remote(look.at[p], look.at[p], lk_send.at[slot], lk_recv.at[slot], tp=pt, kv=pk)

        send(make)
    upto(0, far)
    for relay, finish, came in moves:
        finish()
        source = [xb[q, came].astype(F32) for q in range(TK)]
        square = sum(jnp.sum(v * v, axis=-1, keepdims=True) for v in source)
        scale = lax.rsqrt(square / width + eps)
        for q in range(TK):
            span = slice(q * cols, (q + 1) * cols)
            normed[came, span] = (source[q] * scale * egain[:, span]).astype(BF16)
    upto(0, end)
    upto(1, near)
    local[1].wait()
    local[4].wait()
    settle(0)
    settle(1)
    qs[...] = dot(normed[...], wq[...]).astype(BF16)

    heads = cols // DH
    ratio = cols // kcols
    limit = counts[0] * BLK
    chunk = min(share, length)
    upto(1, far)
    for h in range(heads):
        hs = slice(h * DH, (h + 1) * DH)
        ks = slice(h // ratio * DH, (h // ratio + 1) * DH)
        for c in range(length // chunk):
            lines = slice(c * chunk, (c + 1) * chunk)
            old[h, lines] = jnp.exp(dot_t(qs[lines, hs], hist[0, :, ks]) * DH ** (-0.5))
    upto(1, end)
    local[2].wait()
    settle(2)
    kn[...] = dot(normed[...], wkv[0]).astype(BF16)
    upto(2, near)
    settle(3)
    vn[...] = dot(normed[...], wkv[1]).astype(BF16)

    marks = {1: (2, far), max(heads // 2, 1): (2, end)}
    for h in range(heads):
        hs = slice(h * DH, (h + 1) * DH)
        ks = slice(h // ratio * DH, (h // ratio + 1) * DH)
        for c in range(length // chunk):
            lines = slice(c * chunk, (c + 1) * chunk)
            reach = (c + 1) * chunk
            new = jnp.exp(dot_t(qs[lines, hs], kn[:reach, ks]) * DH ** (-0.5))
            qi = lax.broadcasted_iota(jnp.int32, (chunk, reach), 0) + c * chunk
            ki = lax.broadcasted_iota(jnp.int32, (chunk, reach), 1)
            new = jnp.where((ki <= qi) & (ki < limit), new, 0.0)
            past = old[h, lines]
            total = jnp.sum(past, axis=-1, keepdims=True) + jnp.sum(new, axis=-1, keepdims=True)
            att[lines, hs] = (
                dot((past / total).astype(BF16), hist[1, :, ks])
                + dot((new / total).astype(BF16), vn[:reach, ks])
            ).astype(BF16)
        if h + 1 < heads and h + 1 in marks:
            upto(*marks[h + 1])
    upto(2, end)
    upto(3, near)
    local[5].wait()
    settle(4)
    settle(5)

    def lines_of(which):
        return pl.ds(pl.multiple_of(which * share, share), share)

    def pass_on(c):
        span = slice(c * cols, (c + 1) * cols)
        for i in range(T):
            it = lax.rem(t + 1 + i, T)
            for j in range(1, K):
                piece = rk.at[c, j - 1, i]
                remote(piece, piece, rk_send.at[c, j - 1, i], rk_recv.at[c, j - 1, i], kv=k).wait_recv()
            total = gterm[c, lines_of(it * K + k)].astype(F32)
            for j in range(1, K):
                total = total + rk[c, j - 1, i].astype(F32)
            if i < T - 1:
                s1[c, i] = total.astype(BF16)

                def make(i=i, it=it):
                    return remote(s1.at[c, i], rt.at[c, i], rt_send.at[c, i], rt_recv.at[c, i], tp=it)

                send(make)
            else:
                mixed_ref[:, span] = total

    for c in range(TK):
        gterm[c] = dot_t(att[...], wo[c * cols : (c + 1) * cols, :]).astype(BF16)
        for j in range(1, K):
            pk = lax.rem(k + j, K)
            for i in range(T):

                def make(c=c, j=j, i=i, pk=pk):
                    return remote(
                        gterm.at[c, lines_of(lax.rem(t + 1 + i, T) * K + pk)], rk.at[c, j - 1, i],
                        rk_send.at[c, j - 1, i], rk_recv.at[c, j - 1, i], kv=pk,
                    )

                send(make)
        if c > 0:
            pass_on(c - 1)
    pass_on(TK - 1)
    upto(3, far)
    square = jnp.zeros((share, 1), F32)
    mine = lines_of(p)
    for q in range(TK):
        for i in range(T - 1):
            remote(rt.at[q, i], rt.at[q, i], rt_send.at[q, i], rt_recv.at[q, i], tp=t).wait_recv()
        span = slice(q * cols, (q + 1) * cols)
        value = mixed_ref[:, span]
        for i in range(T - 1):
            value = value + rt[q, i].astype(F32)
        value = value + xb[q, mine].astype(F32)
        mixed_ref[:, span] = value
        square = square + jnp.sum(value * value, axis=-1, keepdims=True)
        enc_out[:, span] = value.astype(BF16)
    scale = lax.rsqrt(square / width + eps)
    cx[p] = (mixed_ref[...] * scale * cgain[...]).astype(BF16)
    relay, finish = spread(cx, S, pl.ds(0, share))
    upto(3, end)

    local[7].wait()
    local[8].wait()
    for slot, other, pt, pk in peers:
        piece = look.at[lax.rem(p - slot - 1 + TK, TK)]
        remote(piece, piece, lk_send.at[slot], lk_recv.at[slot], tp=t).wait_recv()

    def code(level):
        lines = slice(level * beams, (level + 1) * beams)
        return sum(look[q, lines].astype(F32) for q in range(TK))

    def query():
        hidden = hidden_ref[...]
        return dot((hidden * unit(hidden) * dgain[...]).astype(BF16), dq[...]).astype(BF16)

    hidden_ref[...] = code(0)
    queries = query()
    relay()
    local[6].wait()
    settle(6)
    finish()
    across_in = cx[...].reshape(length, width)
    ck[...] = dot(across_in, wc[0]).astype(BF16)
    cv[...] = dot(across_in, wc[1]).astype(BF16)

    live = lax.broadcasted_iota(jnp.int32, (ratio * beams, length), 1) < limit
    for level in range(steps):
        for j in range(kcols // DH):
            ks = slice(j * DH, (j + 1) * DH)
            q = jnp.concatenate(
                [queries[:, (j * ratio + a) * DH : (j * ratio + a + 1) * DH] for a in range(ratio)], axis=0
            )
            raised = jnp.where(live, jnp.exp(dot_t(q, ck[:, ks]) * DH ** (-0.5)), 0.0)
            soft = (raised / jnp.sum(raised, axis=-1, keepdims=True)).astype(BF16)
            found = dot(soft, cv[:, ks]).astype(BF16)
            for a in range(ratio):
                h = j * ratio + a
                ba[:, h * DH : (h + 1) * DH] = found[a * beams : (a + 1) * beams]
        if level < steps - 1:
            for c in range(TK):
                span = slice(c * cols, (c + 1) * cols)
                terms[level, p, :, span] = dot_t(ba[...], do[span, :]).astype(BF16)
            for slot, other, pt, pk in peers:

                def make(slot=slot, pt=pt, pk=pk, level=level):
                    piece = terms.at[level, p]
                    return remote(
                        piece, piece, tm_send.at[level, slot], tm_recv.at[level, slot], tp=pt, kv=pk
                    )

                send(make)
            column = jnp.zeros((beams, 1), jnp.int32)
            line = lax.broadcasted_iota(jnp.int32, column.shape, 0)
            for r in range(beams):
                column = jnp.where(line == r, parents[level, r], column)
            pick = (
                column == lax.broadcasted_iota(jnp.int32, (beams, beams), 1)
            ).astype(F32)
            nextcode = code(level + 1)
            for slot, other, pt, pk in peers:
                piece = terms.at[level, lax.rem(p - slot - 1 + TK, TK)]
                remote(piece, piece, tm_send.at[level, slot], tm_recv.at[level, slot], tp=t).wait_recv()
            state = hidden_ref[...] + sum(terms[level, q].astype(F32) for q in range(TK))
            moved = jnp.dot(pick, state, preferred_element_type=F32, precision=lax.Precision.HIGHEST)
            hidden_ref[...] = moved + nextcode
            queries = query()
        else:
            for c in range(TK):
                span = slice(c * cols, (c + 1) * cols)
                term = dot_t(ba[...], do[span, :])
                last_own[c] = term.astype(BF16)
            for slot, other, pt, pk in peers:

                def make(slot=slot, other=other, pt=pt, pk=pk, level=level):
                    return remote(
                        last_own.at[other], last_in.at[slot],
                        tm_send.at[level, slot], tm_recv.at[level, slot], tp=pt, kv=pk,
                    )

                send(make)
            value = jnp.zeros((beams, cols), F32)
            for c in range(TK):
                span = slice(c * cols, (c + 1) * cols)
                value = jnp.where(p == c, hidden_ref[:, span], value)
            value = value + last_own[p].astype(F32)
            for slot, other, pt, pk in peers:
                piece = last_in.at[slot]
                remote(piece, piece, tm_send.at[level, slot], tm_recv.at[level, slot], tp=t).wait_recv()
            for slot in range(TK - 1):
                value = value + last_in[slot].astype(F32)
            beam_out[...] = value.astype(BF16)

    for make, condition in pending:
        when(condition, lambda make=make: make().wait_send())


def solution(mesh):
    G, S, T, K = (mesh.shape[a] for a in ("groups", "seq", "tp", "kv"))
    TK = T * K

    def shards(
        events, history, counts, ids, parents, wq, wkv, wo, wc, dq, do, table, egain, cgain, dgain
    ):
        users, block, cols = events.shape
        length = block * S
        share = length // TK
        rows, kcols = wkv.shape[1:]
        width = rows * S
        steps, beams = ids.shape
        hist_len = history.shape[2]
        vm = lambda *shape: pltpu.VMEM(shape, BF16)
        vf = lambda *shape: pltpu.VMEM(shape, F32)
        dma = lambda *shape: pltpu.SemaphoreType.DMA(shape)
        anywhere = pl.BlockSpec(memory_space=pl.ANY)
        vmem = pl.BlockSpec(memory_space=pltpu.VMEM)
        smem = pl.BlockSpec(memory_space=pltpu.SMEM)
        enc, beam = pl.pallas_call(
            functools.partial(body, (G, S, T, K)),
            out_shape=(
                jax.ShapeDtypeStruct((share, width), BF16),
                jax.ShapeDtypeStruct((beams, cols), BF16),
            ),
            in_specs=[anywhere, anywhere, smem, smem, smem] + [anywhere] * 7 + [vmem] * 3,
            out_specs=(vmem, vmem),
            scratch_shapes=[
                vm(width, cols), vm(2, width, kcols), vm(width, cols), vm(2, width, kcols),
                vm(width, cols), vm(width, cols), vm(*table.shape), vm(2, hist_len, kcols),
                vm(TK, length, cols), vm(length, width),
                vm(length, cols), vm(length, kcols), vm(length, kcols), vm(length, cols),
                vm(TK, length, cols), vm(TK, max(K - 1, 1), T, share, cols), vm(TK, max(T - 1, 1), share, cols),
                vm(TK, max(T - 1, 1), share, cols), vm(TK, share, width), vm(length, kcols), vm(length, kcols),
                vm(TK, steps * beams, width), vm(steps, TK, beams, width),
                vm(TK, beams, cols), vm(TK, beams, cols),
                vf(beams, width), vf(share, width), vm(beams, cols),
                vf(cols // DH, length, hist_len),
                dma(9), dma(7, 2, S), dma(7, 2, S), dma(7, 2, S, G), dma(7, 2, S, G), dma(S), dma(S),
                dma(S + 1, TK), dma(S + 1, TK), dma(TK), dma(TK), dma(TK, K, T), dma(TK, K, T), dma(TK, T),
                dma(TK, T),
                dma(steps, TK), dma(steps, TK),
            ],
            compiler_params=pltpu.CompilerParams(
                collective_id=0, has_side_effects=True, vmem_limit_bytes=60 * 1024 * 1024
            ),
        )(
            events, history, counts, ids, parents, wq, wkv, wo, wc, dq, do,
            table, egain[None], cgain[None], dgain[None],
        )
        return enc[None], beam

    in_specs = (
        P("groups", "seq", ("tp", "kv")),
        P(None, ("groups", "seq"), None, ("tp", "kv")),
        P(("groups", "seq")),
        P(None, ("groups", "seq")),
        P(None, ("groups", "seq")),
        P("seq", ("tp", "kv")),
        P(None, "seq", ("tp", "kv")),
        P("seq", ("tp", "kv")),
        P(None, "seq", ("tp", "kv")),
        P(None, ("tp", "kv")),
        P(None, ("tp", "kv")),
        P(("tp", "kv"), None),
        P(),
        P(),
        P(),
    )
    out_specs = (P(("groups", "seq"), ("tp", "kv"), None), P(("groups", "seq"), ("tp", "kv")))
    return jax.shard_map(shards, mesh=mesh, in_specs=in_specs, out_specs=out_specs, check_vma=False)
```

profile of v0, /device:TPU:0, one launch (start us, length us, event | category | flops | bytes accessed | tf_op | source)
XLA Modules:
  0.0 139.2 jit_solution(8172007126899402541)
XLA Ops:
  1.3 134.7 %shard_map.158 = (bf16[128,2048]{1,0:T(8,128)(2,1)}, bf16[16,512]{1,0:T(8,128)(2,1)}) custom-call(bf16[4,128,512]{2,1,0:T(8,128)(2,1)} %events.1, bf16[2,1,512,256]{3,2,1,0:T(8,128)(2,1)} %history.1, s32[1]{0:T(128)S(6)} %copy.19.counts, s32[4,16]{1,0:T(4,128)} %ids.1, s32[3,16]{1,0:T(4,128)} %parents.1, bf16[512,512]{1,0:T(8,128)(2,1)} %wq_in.1, ...), custom_call_target="tpu_custom_call" | custom-call | tf_op jit(solution)/shard_map/pallas_call | solution.py:526
  136.0 1.9 %copy.20 = bf16[1,128,2048]{2,1,0:T(8,128)(2,1)} copy(bf16[1,128,2048]{2,1,0:T(8,128)(2,1)} %bitcast.4) | data formatting | bytes 1048576
  137.9 1.3 copy.21
where the time goes:
time: 140 us; the launch traced here: 139 us
  Pallas kernels  135 us (96%)
  local copies, waits for them, and re-layouts  3.2 us (2%)
    pallas_call x1, Pallas kernels, shards(): pl.pallas_call(functools.partial(body, (G, S, T, K)), out_shape=(jax.Shap...  135 us
    unnamed x2, local copies, waits for them, and re-layouts  3.2 us

commit v1 on v0

v1 whole, which is shorter than its diff:
```python
import functools

import jax
import jax.numpy as jnp
from jax import lax
from jax.experimental import pallas as pl
from jax.experimental.pallas import tpu as pltpu
from jax.sharding import PartitionSpec as P

DH = 128
BLK = 128
eps = 1e-06
F32 = jnp.float32
BF16 = jnp.bfloat16
MESH = pl.DeviceIdType.MESH


def unit_of(values):
    return lax.rsqrt(jnp.mean(values * values, axis=-1, keepdims=True) + eps)


def dot(a, b):
    return jnp.dot(a, b, preferred_element_type=F32)


def dot_t(a, b):
    return lax.dot_general(a, b, (((1,), (1,)), ((), ())), preferred_element_type=F32)


def subs_of(planes):
    return (4, 2, 2, 4, 2, 2) if planes <= 4 else (1,) * 6


def body(
    sizes,
    events, history, counts, ids, parents, wq_in, wkv_in, wo_in, wc_in, dq_in, do_in, table_in,
    egain, cgain, dgain,
    enc_out, beam_out,
    wq, wkv, wo, wc, dq, do, table, hist, xb, normed, res, qs, kn, vn, old, pold, pnew, att,
    gterm, rk, s1, rt, acc, cx, sc, ck, cv,
    look_own, look_in, look_sum, look_x, look, terms, last_own, last_in, hidden_ref, ba,
    local_sem, z_send, z_recv, y_send, y_recv, ev_send, ev_recv, xa_send, xa_recv,
    lk_send, lk_recv, rk_send, rk_recv, rt_send, rt_recv, cg_send, cg_recv, sc_send, sc_recv,
    tm_send, tm_recv,
):
    G, S, T, K = sizes
    TK = T * K
    g, s = lax.axis_index("groups"), lax.axis_index("seq")
    t, k = lax.axis_index("tp"), lax.axis_index("kv")
    p = t * K + k
    rows = wq_in.shape[0]
    part = rows // G
    width = wq.shape[0]
    length = normed.shape[0]
    block = length // S
    share = length // TK
    cols = wq.shape[1]
    kcols = kn.shape[1]
    beams = hidden_ref.shape[0]
    steps = ids.shape[0]
    chunks, _, feats = gterm.shape
    half = width // K

    def remote(src, dst, ss, rs, **where):
        return pltpu.make_async_remote_copy(
            src_ref=src, dst_ref=dst, send_sem=ss, recv_sem=rs, device_id=where, device_id_type=MESH
        )

    def wait_recv(ref, sem):
        remote(ref, ref, sem, sem, seq=s).wait_recv()

    def wait_send(ref, sem):
        remote(ref, ref, sem, sem, seq=s).wait_send()

    def inside(z):
        return jnp.logical_and(z >= 0, z < S)

    barrier = pltpu.get_barrier_semaphore()
    for j in range(1, S):
        pl.semaphore_signal(barrier, inc=1, device_id={"seq": lax.rem(s + j, S)}, device_id_type=MESH)
    for j in range(1, G):
        pl.semaphore_signal(barrier, inc=1, device_id={"groups": lax.rem(g + j, G)}, device_id_type=MESH)
    peers = []
    for j in range(1, TK):
        other = lax.rem(p + j, TK)
        peers.append((j - 1, other, lax.div(other, K), lax.rem(other, K)))
        pl.semaphore_signal(
            barrier, inc=1, device_id={"tp": peers[-1][2], "kv": peers[-1][3]}, device_id_type=MESH
        )

    mine = pl.ds(pl.multiple_of(s * rows, rows), rows)
    stay = pl.ds(pl.multiple_of(s * block, block), block)
    local = [
        pltpu.make_async_copy(a, b, local_sem.at[i])
        for i, (a, b) in enumerate(
            [
                (events.at[s], xb.at[p, stay]),
                (table_in, table),
                (wq_in, wq.at[mine]),
                (history.at[:, 0], hist),
                (wkv_in, wkv.at[:, mine]),
                (wo_in, wo.at[mine]),
                (wc_in, wc.at[:, mine]),
                (dq_in, dq),
                (do_in, do),
            ]
        )
    ]
    for copy in local:
        copy.start()
    pl.semaphore_wait(barrier, (S - 1) + (G - 1) + (TK - 1))

    for j in range(1, S):
        to = lax.rem(s + j, S)
        remote(events.at[to], xb.at[p, stay], ev_send.at[0], ev_recv.at[s], seq=to).start()

    weights = [
        (wq, wq_in, None), (wkv, wkv_in, 0), (wkv, wkv_in, 1),
        (wo, wo_in, None), (wc, wc_in, 0), (wc, wc_in, 1),
    ]
    Q, KEY, VALUE, OUT, CKEY, CVALUE = range(6)
    pieces = [(n, sub, of) for n, of in enumerate(subs_of(S)) for sub in range(of)]
    last = {n: i for i, (n, sub, of) in enumerate(pieces)}

    def view(ref, lead, start, size):
        where = pl.ds(pl.multiple_of(start, size), size)
        return ref.at[where] if lead is None else ref.at[lead, where]

    def at(i, origin):
        n, sub, of = pieces[i]
        size = part // of
        return view(weights[n][0], weights[n][2], origin * rows + g * part + sub * size, size)

    def own(i):
        n, sub, of = pieces[i]
        size = part // of
        return view(weights[n][1], weights[n][2], g * part + sub * size, size)

    up = (2 * s) // S
    ways = (2 * up - 1, 1 - 2 * up)

    def forward(i, way, r):
        step = ways[way]
        origin = s - step * r
        src = own(i) if r == 0 else at(i, origin)
        remote(src, at(i, origin), z_send.at[way, r], z_recv.at[i, origin], seq=s + step).start()

    def begin(i):
        for way in (0, 1):
            pl.when(inside(s + ways[way]))(functools.partial(forward, i, way, 0))

    def arrive(i, way, r):
        step = ways[way]
        origin = s - step * r

        def go():
            piece = at(i, origin)
            wait_recv(piece, z_recv.at[i, origin])
            if r + 1 < S:
                pl.when(inside(s + step))(functools.partial(forward, i, way, r))
            for j in range(1, G):
                remote(
                    piece, piece, y_send.at[way, r - 1, j - 1], y_recv.at[pieces[i][0], origin, j - 1],
                    groups=lax.rem(g + j, G),
                ).start()

        pl.when(inside(origin))(go)

    def settle(n, origin):
        def go():
            for j in range(1, G):
                half_of = view(
                    weights[n][0], weights[n][2], origin * rows + lax.rem(g - j + G, G) * part, part
                )
                wait_recv(half_of, y_recv.at[n, origin, j - 1])

        pl.when(origin != s)(go)

    def settle_all(n):
        for origin in range(S):
            settle(n, origin)

    progress = [0]
    AHEAD = 1
    LAG = 1

    def upto(goal):
        while progress[0] <= min(goal, len(pieces) - 1 + (S - 1) * LAG):
            now = progress[0]
            if now == 0:
                for i in range(min(AHEAD, len(pieces))):
                    begin(i)
            if now + AHEAD < len(pieces):
                begin(now + AHEAD)
            for way in (0, 1):
                for r in range(1, S):
                    if 0 <= now - r * LAG < len(pieces):
                        arrive(now - r * LAG, way, r)
            progress[0] += 1

    def arrived(n, r=None):
        upto(last[n] + LAG * (S - 1 if r is None else r))

    unit = part * sum(w[0].shape[-1] for w in weights) // cols

    def finish_weights():
        whole = wq.at[pl.ds(0, unit)]
        for way in (0, 1):
            step = ways[way]
            for r in range(S - 1):
                ok = jnp.logical_and(inside(s + step), inside(s - step * r))
                pl.when(ok)(functools.partial(wait_send, whole, z_send.at[way, r]))
            for r in range(1, S):
                for j in range(1, G):
                    pl.when(inside(s - step * r))(
                        functools.partial(wait_send, whole, y_send.at[way, r - 1, j - 1])
                    )

    def spread(piece_of, send_sem, recv_of):
        def give(source, **where):
            piece = piece_of(source)
            remote(piece, piece, send_sem, recv_of(source), **where).start()

        def take(source):
            wait_recv(piece_of(source), recv_of(source))

        def start():
            for i in range(1, T):
                give(p, tp=lax.rem(t + i, T))
            for j in range(1, K):
                give(p, kv=lax.rem(k + j, K))

        def relay():
            for i in range(1, T):
                there = lax.rem(t - i + T, T) * K + k
                take(there)
                for j in range(1, K):
                    give(there, kv=lax.rem(k + j, K))

        def finish():
            for j in range(1, K):
                for i in range(T):
                    take(lax.rem(t - i + T, T) * K + lax.rem(k - j + K, K))

        return start, relay, finish

    upto(0)

    def came(j):
        return pl.ds(pl.multiple_of(lax.rem(s - j + S, S) * block, block), block)

    moves = [
        spread(lambda q, j=j: xb.at[q, came(j)], xa_send.at[0], lambda q, j=j: xa_recv.at[j, q])
        for j in range(S)
    ]
    local[0].wait()
    moves[0][0]()

    local[1].wait()
    vocab = table.shape[0]
    column = jnp.zeros((steps * beams, 1), jnp.int32)
    line = lax.broadcasted_iota(jnp.int32, column.shape, 0)
    for r in range(steps * beams):
        column = jnp.where(line == r, ids[r // beams, r % beams], column)
    onehot = (
        column == p * vocab + lax.broadcasted_iota(jnp.int32, (steps * beams, vocab), 1)
    ).astype(BF16)
    for kk in range(K):
        for c in range(half // cols if half > cols else 1):
            wide = min(half, cols)
            look_own[kk, :, c * wide : (c + 1) * wide] = dot(
                onehot, table[:, kk * half + c * wide : kk * half + (c + 1) * wide]
            ).astype(BF16)
    for j in range(1, K):
        pk = lax.rem(k + j, K)
        remote(look_own.at[pk], look_in.at[j - 1], lk_send.at[0], lk_recv.at[0, j - 1], kv=pk).start()

    for j in range(1, S):
        wait_recv(xb.at[p, came(j)], ev_recv.at[lax.rem(s - j + S, S)])
        moves[j][0]()
    upto(1)
    moves[0][1]()

    for j in range(1, K):
        wait_recv(look_in.at[j - 1], lk_recv.at[0, j - 1])
    look_sum[...] = (
        look_own[k].astype(F32) + sum(look_in[j].astype(F32) for j in range(K - 1))
    ).astype(BF16)
    for i in range(1, T):
        remote(
            look_sum, look_x.at[i - 1], lk_send.at[1], lk_recv.at[1, i - 1], tp=lax.rem(t + i, T)
        ).start()

    for j in range(1, S):
        moves[j][1]()
    upto(2)
    for j in range(S):
        moves[j][2]()
        lines = came(j)
        source = [xb[q, lines].astype(F32) for q in range(TK)]
        square = sum(jnp.sum(v * v, axis=-1, keepdims=True) for v in source)
        scale = lax.rsqrt(square / width + eps)
        for q in range(TK):
            span = slice(q * cols, (q + 1) * cols)
            normed[lines, span] = (source[q] * scale * egain[:, span]).astype(BF16)
        if j == S // 2:
            upto(3)

    def lines_of(which):
        return pl.ds(pl.multiple_of(which * share, share), share)

    for q in range(TK):
        res[:, q * cols : (q + 1) * cols] = xb[q, lines_of(p)]
    for i in range(1, T):
        wait_recv(look_x.at[i - 1], lk_recv.at[1, i - 1])
    look[k] = (
        look_sum[...].astype(F32) + sum(look_x[i].astype(F32) for i in range(T - 1))
    ).astype(BF16)
    for j in range(1, K):
        remote(look.at[k], look.at[k], lk_send.at[2], lk_recv.at[2, j - 1], kv=lax.rem(k + j, K)).start()
    upto(4)
    for j in range(1, K):
        wait_recv(look.at[lax.rem(k - j + K, K)], lk_recv.at[2, j - 1])

    def code(level):
        lines = slice(level * beams, (level + 1) * beams)
        return jnp.concatenate([look[kk, lines] for kk in range(K)], axis=-1).astype(F32)

    def query(hidden):
        raw = dot((hidden * dgain[...]).astype(BF16), dq[...])
        return (raw * unit_of(hidden)).astype(BF16)

    local[7].wait()
    hidden_ref[...] = code(0)
    queries = query(hidden_ref[...])
    upto(5)

    local[2].wait()
    arrived(Q)
    settle_all(Q)
    qs[...] = dot(normed[...], wq[...]).astype(BF16)

    heads = cols // DH
    ratio = cols // kcols
    limit = counts[0] * BLK
    chunk = min(share, length)
    local[3].wait()
    for h in range(heads):
        hs = slice(h * DH, (h + 1) * DH)
        ks = slice(h // ratio * DH, (h // ratio + 1) * DH)
        for c in range(length // chunk):
            lines = slice(c * chunk, (c + 1) * chunk)
            old[h, lines] = jnp.exp(dot_t(qs[lines, hs], hist[0, :, ks]) * DH ** (-0.5))
        if h == heads // 2 - 1:
            upto(last[Q] + (S - 1) * LAG + 1)
    local[4].wait()
    arrived(KEY)
    settle_all(KEY)
    kn[...] = dot(normed[...], wkv[0]).astype(BF16)
    for h in range(heads):
        hs = slice(h * DH, (h + 1) * DH)
        ks = slice(h // ratio * DH, (h // ratio + 1) * DH)
        for c in range(length // chunk):
            lines = slice(c * chunk, (c + 1) * chunk)
            reach = (c + 1) * chunk
            new = jnp.exp(dot_t(qs[lines, hs], kn[:reach, ks]) * DH ** (-0.5))
            qi = lax.broadcasted_iota(jnp.int32, (chunk, reach), 0) + c * chunk
            ki = lax.broadcasted_iota(jnp.int32, (chunk, reach), 1)
            new = jnp.where((ki <= qi) & (ki < limit), new, 0.0)
            past = old[h, lines]
            total = jnp.sum(past, axis=-1, keepdims=True) + jnp.sum(new, axis=-1, keepdims=True)
            pold[h, lines] = (past / total).astype(BF16)
            pnew[h, lines, :reach] = (new / total).astype(BF16)
        if h == heads // 2 - 1:
            upto(last[KEY] + (S - 1) * LAG + 1)
    arrived(VALUE)
    settle_all(VALUE)
    vn[...] = dot(normed[...], wkv[1]).astype(BF16)
    for h in range(heads):
        hs = slice(h * DH, (h + 1) * DH)
        ks = slice(h // ratio * DH, (h // ratio + 1) * DH)
        for c in range(length // chunk):
            lines = slice(c * chunk, (c + 1) * chunk)
            reach = (c + 1) * chunk
            att[lines, hs] = (
                dot(pold[h, lines], hist[1, :, ks]) + dot(pnew[h, lines, :reach], vn[:reach, ks])
            ).astype(BF16)
    local[5].wait()

    in_turn = chunks == S and S & (S - 1) == 0

    def features(i):
        if not in_turn:
            return i
        at_plane, bit = 0, 1
        while bit < S:
            here = lax.rem(lax.div(s, bit), 2)
            at_plane = at_plane + bit * (1 - here if i & bit else here)
            bit *= 2
        return at_plane

    def span_of(i):
        return pl.ds(pl.multiple_of(features(i) * feats, feats), feats)

    def project(i):
        gterm[i] = dot_t(att[...], wo[span_of(i), :]).astype(BF16)
        for j in range(1, K):
            pk = lax.rem(k + j, K)
            for it in range(T):
                remote(
                    gterm.at[i, lines_of(lax.rem(t + 1 + it, T) * K + pk)], rk.at[i, j - 1, it],
                    rk_send.at[0], rk_recv.at[i, j - 1], kv=pk,
                ).start()

    def pass_on(i):
        for j in range(1, K):
            wait_recv(rk.at[i, j - 1], rk_recv.at[i, j - 1])
        for it in range(T):
            to = lax.rem(t + 1 + it, T)
            total = gterm[i, lines_of(to * K + k)].astype(F32)
            for j in range(1, K):
                total = total + rk[i, j - 1, it].astype(F32)
            if it < T - 1:
                s1[i, it] = total.astype(BF16)
                remote(s1.at[i, it], rt.at[i, it], rt_send.at[0], rt_recv.at[i, it], tp=to).start()
            else:
                acc[i] = total

    gathers = [
        spread(
            lambda q, i=i: cx.at[features(i), lines_of(q)], cg_send.at[0], lambda q, i=i: cg_recv.at[i, q]
        )
        for i in range(chunks)
    ]
    squares = []

    def complete(i):
        value = acc[i]
        for it in range(T - 1):
            wait_recv(rt.at[i, it], rt_recv.at[i, it])
            value = value + rt[i, it].astype(F32)
        value = value + res[:, span_of(i)].astype(F32)
        squares.append(jnp.sum(value * value, axis=-1, keepdims=True))
        cx[features(i), lines_of(p)] = (value * cgain[:, span_of(i)]).astype(BF16)
        gathers[i][0]()
        enc_out[:, span_of(i)] = value.astype(BF16)

    if not in_turn:
        arrived(OUT)
        settle_all(OUT)
    for i in range(chunks + 5):
        if i < chunks:
            if in_turn:
                arrived(OUT, i)
                if i > 0:
                    settle(OUT, features(i))
            project(i)
        else:
            upto(last[OUT] + (S - 1) * LAG + 1 + i - chunks)
        if 1 <= i < chunks + 1:
            pass_on(i - 1)
        if 2 <= i < chunks + 2:
            complete(i - 2)
            if i == chunks + 2 - 1:
                scale = lax.rsqrt(sum(squares) / width + eps)
                sc[p] = jnp.broadcast_to(scale, (share, 128))
                for slot, other, pt, pk in peers:
                    remote(sc.at[p], sc.at[p], sc_send.at[0], sc_recv.at[p], tp=pt, kv=pk).start()
        if 4 <= i < chunks + 4:
            gathers[i - 4][1]()
    arrived(CKEY)
    for slot, other, pt, pk in peers:
        wait_recv(sc.at[other], sc_recv.at[other])
    for start, relay, finish in gathers:
        finish()
    local[6].wait()
    settle_all(CKEY)
    by_row = sc[...].reshape(length, 128)[:, :1]

    def across(which):
        total = dot(cx[0], wc[which, :feats])
        for c in range(1, chunks):
            total = total + dot(cx[c], wc[which, c * feats : (c + 1) * feats])
        return (total * by_row).astype(BF16)

    ck[...] = across(0)
    live = lax.broadcasted_iota(jnp.int32, (ratio * beams, length), 1) < limit

    def soften(queries, j):
        ks = slice(j * DH, (j + 1) * DH)
        q = jnp.concatenate(
            [queries[:, (j * ratio + a) * DH : (j * ratio + a + 1) * DH] for a in range(ratio)], axis=0
        )
        raised = jnp.where(live, jnp.exp(dot_t(q, ck[:, ks]) * DH ** (-0.5)), 0.0)
        return (raised / jnp.sum(raised, axis=-1, keepdims=True)).astype(BF16)

    soft = [soften(queries, j) for j in range(kcols // DH)]
    local[8].wait()
    arrived(CVALUE)
    settle_all(CVALUE)
    cv[...] = across(1)

    for level in range(steps):
        if level > 0:
            soft = [soften(queries, j) for j in range(kcols // DH)]
        for j in range(kcols // DH):
            ks = slice(j * DH, (j + 1) * DH)
            found = dot(soft[j], cv[:, ks]).astype(BF16)
            for a in range(ratio):
                h = j * ratio + a
                ba[:, h * DH : (h + 1) * DH] = found[a * beams : (a + 1) * beams]
        if level < steps - 1:
            column = jnp.zeros((beams, 1), jnp.int32)
            line = lax.broadcasted_iota(jnp.int32, column.shape, 0)
            for r in range(beams):
                column = jnp.where(line == r, parents[level, r], column)
            pick = column == lax.broadcasted_iota(jnp.int32, (beams, beams), 1)
            picked = dot(pick.astype(BF16), ba[...]).astype(BF16)
            for c in range(TK):
                terms[level, p, c] = dot_t(picked, do[c * cols : (c + 1) * cols, :]).astype(BF16)
                for slot, other, pt, pk in peers:
                    piece = terms.at[level, p, c]
                    remote(piece, piece, tm_send.at[0], tm_recv.at[level, p], tp=pt, kv=pk).start()
            moved = jnp.dot(
                pick.astype(F32), hidden_ref[...], preferred_element_type=F32, precision=lax.Precision.HIGHEST
            )
            hidden_ref[...] = moved + code(level + 1)
            for slot, other, pt, pk in peers:
                wait_recv(terms.at[level, other], tm_recv.at[level, other])
            for c in range(TK):
                span = slice(c * cols, (c + 1) * cols)
                hidden_ref[:, span] = hidden_ref[:, span] + sum(
                    terms[level, q, c].astype(F32) for q in range(TK)
                )
            queries = query(hidden_ref[...])
        else:
            for c in range(TK):
                last_own[c] = dot_t(ba[...], do[c * cols : (c + 1) * cols, :]).astype(BF16)
            for slot, other, pt, pk in peers:
                remote(
                    last_own.at[other], last_in.at[slot], tm_send.at[1], tm_recv.at[level, slot], tp=pt, kv=pk
                ).start()
            value = jnp.zeros((beams, cols), F32)
            for c in range(TK):
                span = slice(c * cols, (c + 1) * cols)
                value = jnp.where(p == c, hidden_ref[:, span], value)
            value = value + last_own[p].astype(F32)
            for slot, other, pt, pk in peers:
                wait_recv(last_in.at[slot], tm_recv.at[level, slot])
            for slot in range(TK - 1):
                value = value + last_in[slot].astype(F32)
            beam_out[...] = value.astype(BF16)

    finish_weights()
    wait_send(xb.at[0, pl.ds(0, (S - 1) * block)], ev_send.at[0])
    wait_send(xb.at[pl.ds(0, TK - 1)], xa_send.at[0])
    wait_send(look_in, lk_send.at[0])
    wait_send(look_x, lk_send.at[1])
    wait_send(look_in, lk_send.at[2])
    wait_send(rk, rk_send.at[0])
    wait_send(rt, rt_send.at[0])
    wait_send(cx.at[:, pl.ds(0, (TK - 1) * share)], cg_send.at[0])
    wait_send(sc.at[pl.ds(0, TK - 1)], sc_send.at[0])
    wait_send(terms.at[pl.ds(0, steps - 1), pl.ds(0, TK - 1)], tm_send.at[0])
    wait_send(last_in, tm_send.at[1])


def solution(mesh):
    G, S, T, K = (mesh.shape[a] for a in ("groups", "seq", "tp", "kv"))
    TK = T * K

    def shards(
        events, history, counts, ids, parents, wq, wkv, wo, wc, dq, do, table, egain, cgain, dgain
    ):
        users, block, cols = events.shape
        length = block * S
        share = length // TK
        rows, kcols = wkv.shape[1:]
        width = rows * S
        steps, beams = ids.shape
        hist_len = history.shape[2]
        heads = cols // DH
        chunks = S if rows % 128 == 0 else TK
        feats = width // chunks
        pieces = sum(subs_of(S))
        vm = lambda *shape: pltpu.VMEM(shape, BF16)
        vf = lambda *shape: pltpu.VMEM(shape, F32)
        dma = lambda *shape: pltpu.SemaphoreType.DMA(shape)
        anywhere = pl.BlockSpec(memory_space=pl.ANY)
        vmem = pl.BlockSpec(memory_space=pltpu.VMEM)
        smem = pl.BlockSpec(memory_space=pltpu.SMEM)
        enc, beam = pl.pallas_call(
            functools.partial(body, (G, S, T, K)),
            out_shape=(
                jax.ShapeDtypeStruct((share, width), BF16),
                jax.ShapeDtypeStruct((beams, cols), BF16),
            ),
            in_specs=[anywhere, anywhere, smem, smem, smem] + [anywhere] * 7 + [vmem] * 3,
            out_specs=(vmem, vmem),
            scratch_shapes=[
                vm(width, cols), vm(2, width, kcols), vm(width, cols), vm(2, width, kcols),
                vm(width, cols), vm(width, cols), vm(*table.shape), vm(2, hist_len, kcols),
                vm(TK, length, cols), vm(length, width), vm(share, width),
                vm(length, cols), vm(length, kcols), vm(length, kcols),
                vf(heads, length, hist_len), vm(heads, length, hist_len), vm(heads, length, length),
                vm(length, cols),
                vm(chunks, length, feats), vm(chunks, K - 1, T, share, feats),
                vm(chunks, T - 1, share, feats), vm(chunks, T - 1, share, feats),
                vf(chunks, share, feats), vm(chunks, length, feats), vf(TK, share, 128),
                vm(length, kcols), vm(length, kcols),
                vm(K, steps * beams, width // K), vm(K - 1, steps * beams, width // K),
                vm(steps * beams, width // K), vm(T - 1, steps * beams, width // K),
                vm(K, steps * beams, width // K),
                vm(steps - 1, TK, TK, beams, cols), vm(TK, beams, cols), vm(TK - 1, beams, cols),
                vf(beams, width), vm(beams, cols),
                dma(9), dma(2, S - 1), dma(pieces, S), dma(2, S - 1, G - 1), dma(6, S, G - 1),
                dma(1), dma(S), dma(1), dma(S, TK),
                dma(3), dma(3, max(T, K) - 1), dma(1), dma(chunks, K - 1), dma(1), dma(chunks, T - 1),
                dma(1), dma(chunks, TK), dma(1), dma(TK),
                dma(2), dma(steps, TK),
            ],
            compiler_params=pltpu.CompilerParams(
                collective_id=0, has_side_effects=True, vmem_limit_bytes=60 * 1024 * 1024
            ),
        )(
            events, history, counts, ids, parents, wq, wkv, wo, wc, dq, do,
            table, egain[None], cgain[None], dgain[None],
        )
        return enc[None], beam

    in_specs = (
        P("groups", "seq", ("tp", "kv")),
        P(None, ("groups", "seq"), None, ("tp", "kv")),
        P(("groups", "seq")),
        P(None, ("groups", "seq")),
        P(None, ("groups", "seq")),
        P("seq", ("tp", "kv")),
        P(None, "seq", ("tp", "kv")),
        P("seq", ("tp", "kv")),
        P(None, "seq", ("tp", "kv")),
        P(None, ("tp", "kv")),
        P(None, ("tp", "kv")),
        P(("tp", "kv"), None),
        P(),
        P(),
        P(),
    )
    out_specs = (P(("groups", "seq"), ("tp", "kv"), None), P(("groups", "seq"), ("tp", "kv")))
    return jax.shard_map(shards, mesh=mesh, in_specs=in_specs, out_specs=out_specs, check_vma=False)
```

time: 140 us -> 137 us (0.979)
  Pallas kernels: 135 us -> 132 us
    pallas_call x1, Pallas kernels: 135 us -> 132 us  [shards(): pl.pallas_call(functools.partial(body, (G, S, T, K)), out_shape=(jax.Shap...]
where the time goes in v1:
time: 137 us
  Pallas kernels  132 us (96%)
  local copies, waits for them, and re-layouts  3.2 us (2%)
    pallas_call x1, Pallas kernels, shards(): pl.pallas_call(functools.partial(body, (G, S, T, K)), out_shape=(jax.Shap...  132 us
    unnamed x2, local copies, waits for them, and re-layouts  3.2 us

profile of v1, /device:TPU:0, one launch (start us, length us, event | category | flops | bytes accessed | tf_op | source)
XLA Modules:
  0.0 136.9 jit_solution(8403183762778307427)
XLA Ops:
  1.3 132.4 %shard_map.158 = (bf16[128,2048]{1,0:T(8,128)(2,1)}, bf16[16,512]{1,0:T(8,128)(2,1)}) custom-call(bf16[4,128,512]{2,1,0:T(8,128)(2,1)} %events.1, bf16[2,1,512,256]{3,2,1,0:T(8,128)(2,1)} %history.1, s32[1]{0:T(128)S(6)} %copy.19.counts, s32[4,16]{1,0:T(4,128)} %ids.1, s32[3,16]{1,0:T(4,128)} %parents.1, bf16[512,512]{1,0:T(8,128)(2,1)} %wq_in.1, ...), custom_call_target="tpu_custom_call" | custom-call | tf_op jit(solution)/shard_map/pallas_call | solution.py:592
  133.7 1.9 %copy.20 = bf16[1,128,2048]{2,1,0:T(8,128)(2,1)} copy(bf16[1,128,2048]{2,1,0:T(8,128)(2,1)} %bitcast.4) | data formatting | bytes 1048576
  135.6 1.3 copy.21

commit v2 on v1

--- a/solution.py
+++ b/solution.py
@@ -193,7 +193,7 @@
             if now + AHEAD < len(pieces):
                 begin(now + AHEAD)
             for way in (0, 1):
-                for r in range(1, S):
+                for r in reversed(range(1, S)):
                     if 0 <= now - r * LAG < len(pieces):
                         arrive(now - r * LAG, way, r)
             progress[0] += 1
@@ -518,9 +518,9 @@
             picked = dot(pick.astype(BF16), ba[...]).astype(BF16)
             for c in range(TK):
                 terms[level, p, c] = dot_t(picked, do[c * cols : (c + 1) * cols, :]).astype(BF16)
-                for slot, other, pt, pk in peers:
-                    piece = terms.at[level, p, c]
-                    remote(piece, piece, tm_send.at[0], tm_recv.at[level, p], tp=pt, kv=pk).start()
+            for slot, other, pt, pk in reversed(peers):
+                piece = terms.at[level, p]
+                remote(piece, piece, tm_send.at[0], tm_recv.at[level, p], tp=pt, kv=pk).start()
             moved = jnp.dot(
                 pick.astype(F32), hidden_ref[...], preferred_element_type=F32, precision=lax.Precision.HIGHEST
             )

time: 137 us -> 132 us (0.964)
  Pallas kernels: 132 us -> 128 us
    pallas_call x1, Pallas kernels: 132 us -> 128 us  [shards(): pl.pallas_call(functools.partial(body, (G, S, T, K)), out_shape=(jax.Shap...]
where the time goes in v2:
time: 132 us
  Pallas kernels  128 us (97%)
  local copies, waits for them, and re-layouts  3.2 us (2%)
    pallas_call x1, Pallas kernels, shards(): pl.pallas_call(functools.partial(body, (G, S, T, K)), out_shape=(jax.Shap...  128 us
    unnamed x2, local copies, waits for them, and re-layouts  3.2 us

profile of v2, /device:TPU:0, one launch (start us, length us, event | category | flops | bytes accessed | tf_op | source)
XLA Modules:
  0.0 132.1 jit_solution(17187747128974863010)
XLA Ops:
  1.3 127.6 %shard_map.158 = (bf16[128,2048]{1,0:T(8,128)(2,1)}, bf16[16,512]{1,0:T(8,128)(2,1)}) custom-call(bf16[4,128,512]{2,1,0:T(8,128)(2,1)} %events.1, bf16[2,1,512,256]{3,2,1,0:T(8,128)(2,1)} %history.1, s32[1]{0:T(128)S(6)} %copy.19.counts, s32[4,16]{1,0:T(4,128)} %ids.1, s32[3,16]{1,0:T(4,128)} %parents.1, bf16[512,512]{1,0:T(8,128)(2,1)} %wq_in.1, ...), custom_call_target="tpu_custom_call" | custom-call | tf_op jit(solution)/shard_map/pallas_call | solution.py:592
  128.8 1.9 %copy.20 = bf16[1,128,2048]{2,1,0:T(8,128)(2,1)} copy(bf16[1,128,2048]{2,1,0:T(8,128)(2,1)} %bitcast.4) | data formatting | bytes 1048576
  130.7 1.3 %copy.21 = bf16[16,512]{1,0:T(8,128)(2,1)} copy(bf16[16,512]{1,0:T(8,128)(2,1)} %get-tuple-element.9) | data formatting | bytes 32768
